TPU v7x, 32 devices: a whole 2x2x4 slice. The times are simulated.
32 devices in a mesh: seg: 4 (over y, x), slab: 8 (over z, core).
Axes of the slice: x: 2, y: 2, z: 4, core: 2. Of those that a mesh axis runs over, the one named last changes fastest.
Arguments:
- positions: bfloat16 [4, 32, 3, 642], P('seg', 'slab'), may hold values from -6 to 6
- density: bfloat16 [4, 32, 3, 642], P('seg', 'slab'), may hold values from -6 to 6
- upsample: bfloat16 [642, 2562], replicated, may hold values from -0.25 to 0.25
- quad_weights: float32 [2562], replicated, may hold values from 0.3 to 3
- coarse_weights: float32 [642], replicated, may hold values from 0.3 to 3
- pair_target: int32 [4, 16], P('seg', 'slab'), may hold values from 0 to 3
- pair_source: int32 [4, 16], P('seg', 'slab'), may hold values from 0 to 7
- junction_cell: int32 [4, 8, 4], P('seg', 'slab'), may hold values from 0 to 3
- junction_target: int32 [4, 8, 4], P('seg', 'slab'), may hold values from 0 to 3
- wall_points: bfloat16 [4, 8, 3, 128], P('seg', 'slab'), may hold values from -6 to 6
- wall_traction: bfloat16 [4, 8, 3, 128], P('seg', 'slab'), may hold values from -6 to 6
- wall_near: int32 [4, 32, 2], P('seg', 'slab'), may hold values from 0 to 7
Outputs:
- velocity: float32 [4, 32, 3, 642], P('seg', 'slab')
All inputs are finite; a program needn't handle non-finite values.
Results may differ from a plain program's by a relative error of at most 0.0024.
Values may be sent and summed in bfloat16 or wider, within the bound.
A program may use at most 64 MiB of HBM per device.

v0:
```python
import math

import jax
import jax.numpy as jnp
from jax import lax
from jax.sharding import PartitionSpec as P

HALO = 2


EPSILON2 = 0.05
WALL_GAIN = 3.0


def with_halo(block, sides, width):
    for axis, dim in sides:
        count = lax.axis_size(axis)
        forward = [(i, i + 1) for i in range(count - 1)]
        backward = [(target, source) for source, target in forward]
        low = lax.ppermute(
            lax.slice_in_dim(block, block.shape[dim] - width, None, axis=dim), axis, forward
        )
        high = lax.ppermute(lax.slice_in_dim(block, 0, width, axis=dim), axis, backward)
        block = jnp.concatenate([low, block, high], axis=dim)
    return block


def kernel_rows(targets, sources, strength):
    offset = targets[:, :, None] - sources[:, None, :]
    distance2 = jnp.sum(offset * offset, axis=0)
    inverse = lax.rsqrt(distance2 + EPSILON2)
    inverse3 = inverse * inverse * inverse
    along_offset = jnp.sum(offset * strength[:, None, :], axis=0)
    summand = (
        strength[:, None, :] * (distance2 + 2.0 * EPSILON2) + along_offset[None] * offset
    ) * inverse3[None]
    return jnp.sum(summand, axis=2) / (8.0 * math.pi)


def stokes_block(targets, sources, strength):
    points = targets.shape[1]
    blocked = targets.reshape(3, 6, points // 6).transpose(1, 0, 2)
    result = lax.map(lambda target_rows: kernel_rows(target_rows, sources, strength), blocked)
    return result.transpose(1, 0, 2).reshape(3, points)


def add_to_cells(blocks, index, cell_count):
    onehot = (index[None, :] == jnp.arange(cell_count, dtype=jnp.int32)[:, None]).astype(
        jnp.float32
    )
    return jnp.einsum("cn,nkp->ckp", onehot, blocks, precision=lax.Precision.HIGHEST)


def local(
    positions,
    density,
    upsample,
    quad_weights,
    coarse_weights,
    pair_target,
    pair_source,
    junction_cell,
    junction_target,
    wall_points,
    wall_traction,
    wall_near,
):
    coarse_pos = positions[0]
    coarse_den = density[0]
    cell_count = coarse_pos.shape[0]
    rim_pos, rim_den = (
        with_halo(coarse_pos, (("slab", 0),), HALO),
        with_halo(coarse_den, (("slab", 0),), HALO),
    )
    fine_pos = jnp.einsum(
        "ckp,pq->ckq", rim_pos, upsample, preferred_element_type=jnp.float32
    ).astype(jnp.bfloat16)
    fine_den = jnp.einsum(
        "ckp,pq->ckq", rim_den, upsample, preferred_element_type=jnp.float32
    ).astype(jnp.bfloat16)
    targets = pair_target[0]
    sources = pair_source[0]

    def fine_pair(operands):
        target_pts, source_pts, source_den = operands
        strength = source_den.astype(jnp.float32) * quad_weights[None, :]
        return stokes_block(
            target_pts.astype(jnp.float32), source_pts.astype(jnp.float32), strength
        )

    local_blocks = lax.map(fine_pair, (coarse_pos[targets], fine_pos[sources], fine_den[sources]))
    velocity = add_to_cells(local_blocks, targets, cell_count)
    chosen = junction_cell[0, 0]
    arrived_pos, arrived_den = (
        lax.all_to_all(coarse_pos[chosen], "seg", split_axis=0, concat_axis=0, tiled=True),
        lax.all_to_all(coarse_den[chosen], "seg", split_axis=0, concat_axis=0, tiled=True),
    )
    goals = junction_target[0, 0]
    alive_mask = (jnp.arange(goals.shape[0], dtype=jnp.int32) != lax.axis_index("seg")).astype(
        jnp.float32
    )

    def coarse_pair(operands):
        target_pts, source_pts, source_den = operands
        strength = source_den.astype(jnp.float32) * coarse_weights[None, :]
        return stokes_block(
            target_pts.astype(jnp.float32), source_pts.astype(jnp.float32), strength
        )

    junction_blocks = (
        lax.map(coarse_pair, (coarse_pos[goals], arrived_pos, arrived_den))
        * alive_mask[:, None, None]
    )
    velocity = velocity + add_to_cells(junction_blocks, goals, cell_count)
    patch_pos, patch_trac = (
        lax.all_gather(wall_points[0], "slab", axis=0, tiled=True),
        lax.all_gather(wall_traction[0], "slab", axis=0, tiled=True),
    )
    near_rows = wall_near[0].reshape(-1)
    near_count = wall_near.shape[2]

    def wall_pair(operands):
        target_pts, source_pts, source_den = operands
        return stokes_block(
            target_pts.astype(jnp.float32),
            source_pts.astype(jnp.float32),
            source_den.astype(jnp.float32) * WALL_GAIN,
        )

    wall_blocks = lax.map(
        wall_pair,
        (jnp.repeat(coarse_pos, near_count, axis=0), patch_pos[near_rows], patch_trac[near_rows]),
    )
    velocity = velocity + jnp.sum(
        wall_blocks.reshape((cell_count, near_count) + wall_blocks.shape[1:]), axis=1
    )
    return velocity[None]


def solution(mesh):
    placed = (
        P("seg", "slab", None, None),
        P("seg", "slab", None, None),
        P(),
        P(),
        P(),
        P("seg", "slab"),
        P("seg", "slab"),
        P("seg", "slab", None),
        P("seg", "slab", None),
        P("seg", "slab", None, None),
        P("seg", "slab", None, None),
        P("seg", "slab", None),
    )
    return jax.shard_map(
        local, mesh=mesh, in_specs=placed, out_specs=P("seg", "slab", None, None), check_vma=False
    )
```

profile of v0, /device:TPU:0, one launch (start us, length us, event | category | flops | bytes accessed | tf_op | source)
XLA Modules:
  0.0 205.6 jit_solution(8631033830005076879)
XLA Ops:
  0.0 1.5 slice_bitcast_fusion.3
  1.5 3.0 %collective-permute-start = (bf16[2,3,642]{2,0,1:T(2,128)(2,1)}, bf16[2,3,642]{2,0,1:T(2,128)(2,1)}, u32[]{:S(2)}, u32[]{:S(2)}) collective-permute-start(bf16[2,3,642]{2,0,1:T(2,128)(2,1)} %get-tuple-element.324), channel_id=1, source_target_pairs={{0,1},{1,2},{2,3},{3,4},{4,5},{5,6},{6,7},{8,9},{9,10},{10,11},{11... | collective-permute-start | bytes 23120 | tf_op jit(solution)/shard_map/ppermute | solution.py:20
  5.8 1.4 slice_bitcast_fusion.1
  7.2 5.2 %collective-permute-start.2 = (bf16[2,3,642]{2,0,1:T(2,128)(2,1)}, bf16[2,3,642]{2,0,1:T(2,128)(2,1)}, u32[]{:S(2)}, u32[]{:S(2)}) collective-permute-start(bf16[2,3,642]{2,0,1:T(2,128)(2,1)} %get-tuple-element.322), channel_id=1, source_target_pairs={{0,1},{1,2},{2,3},{3,4},{4,5},{5,6},{6,7},{8,9},{9,10},{10,11},{11... | collective-permute-start | bytes 23120 | tf_op jit(solution)/shard_map/ppermute | solution.py:20
  16.3 3.9 %all-to-all-start = ((bf16[4,3,642]{2,1,0:T(4,128)(2,1)}), bf16[4,3,642]{2,1,0:T(4,128)(2,1)}, u32[]{:S(2)}, u32[]{:S(2)}) async-start(bf16[4,3,642]{2,1,0:T(4,128)(2,1)} %gather_fusion.4), calls=%async_computation | async-start | bytes 49152 | tf_op jit(solution)/shard_map/all_to_all | solution.py:95
  24.8 14.1 %all-gather = bf16[8,1,3,128]{3,2,1,0:T(4,128)(2,1)S(1)} all-gather(bf16[1,1,3,128]{3,2,1,0:T(4,128)(2,1)} %param.33), channel_id=2, replica_groups=mesh['seg'=4,'slab'=8] {'slab'}, dimensions={0}, use_global_device_ids=true | all-gather | bytes 6912 | tf_op jit(solution)/shard_map/all_gather | solution.py:116
  38.9 9.0 %all-gather.1 = bf16[8,1,3,128]{3,2,1,0:T(4,128)(2,1)S(1)} all-gather(bf16[1,1,3,128]{3,2,1,0:T(4,128)(2,1)} %param.34), channel_id=3, replica_groups=mesh['seg'=4,'slab'=8] {'slab'}, dimensions={0}, use_global_device_ids=true | all-gather | bytes 6912 | tf_op jit(solution)/shard_map/all_gather | solution.py:117
  50.2 37.8 %while.65 = (s32[]{:T(128)}, f32[8,3,642]{2,1,0:T(4,128)}, bf16[8,3,642]{2,1,0:T(4,128)(2,1)}, bf16[8,3,128]{2,1,0:T(4,128)(2,1)S(1)}, bf16[8,3,128]{2,1,0:T(4,128)(2,1)}, /*index=5*/s32[]{:T(128)}, s32[]{:T(128)}, s32[]{:T(128)}) while((s32[]{:T(128)}, f32[8,3,642]{2,1,0:T(4,128)}, bf16[8,3,642]{2,1,0:T(4,128)(2,1)}, ...), condition=%wide.region_20.21_spmd, body=%wide.region_14.20_spmd.sunk | while | flops 482442 | bytes 540622 | solution.py:130
  51.6 2.6 %while.68 = (s32[]{:T(128)}, f32[6,3,107]{2,1,0:T(4,128)S(1)}, f32[3,128]{1,0:T(4,128)S(1)}, f32[6,3,107]{2,0,1:T(8,128)S(1)}, f32[3,128]{1,0:T(4,128)S(1)}, /*index=5*/s32[]{:T(128)}) while((s32[]{:T(128)}, f32[6,3,107]{2,1,0:T(4,128)S(1)}, f32[3,128]{1,0:T(4,128)S(1)}, f32[6,3,107]{2,0,1:T(8,128)S(1)}, f32[3,128]{1,0:T(4,128)S(1)}, ...), condition=%wide.region_19.19_spmd, body=%wide.region_15.18_spmd.sunk | while | flops 479362 | bytes 457577 | solution.py:43
  56.4 2.6 %while.68 = (s32[]{:T(128)}, f32[6,3,107]{2,1,0:T(4,128)S(1)}, f32[3,128]{1,0:T(4,128)S(1)}, f32[6,3,107]{2,0,1:T(8,128)S(1)}, f32[3,128]{1,0:T(4,128)S(1)}, /*index=5*/s32[]{:T(128)}) while((s32[]{:T(128)}, f32[6,3,107]{2,1,0:T(4,128)S(1)}, f32[3,128]{1,0:T(4,128)S(1)}, f32[6,3,107]{2,0,1:T(8,128)S(1)}, f32[3,128]{1,0:T(4,128)S(1)}, ...), condition=%wide.region_19.19_spmd, body=%wide.region_15.18_spmd.sunk | while | flops 479362 | bytes 457577 | solution.py:43
  61.1 2.6 %while.68 = (s32[]{:T(128)}, f32[6,3,107]{2,1,0:T(4,128)S(1)}, f32[3,128]{1,0:T(4,128)S(1)}, f32[6,3,107]{2,0,1:T(8,128)S(1)}, f32[3,128]{1,0:T(4,128)S(1)}, /*index=5*/s32[]{:T(128)}) while((s32[]{:T(128)}, f32[6,3,107]{2,1,0:T(4,128)S(1)}, f32[3,128]{1,0:T(4,128)S(1)}, f32[6,3,107]{2,0,1:T(8,128)S(1)}, f32[3,128]{1,0:T(4,128)S(1)}, ...), condition=%wide.region_19.19_spmd, body=%wide.region_15.18_spmd.sunk | while | flops 479362 | bytes 457577 | solution.py:43
  65.8 2.6 %while.68 = (s32[]{:T(128)}, f32[6,3,107]{2,1,0:T(4,128)S(1)}, f32[3,128]{1,0:T(4,128)S(1)}, f32[6,3,107]{2,0,1:T(8,128)S(1)}, f32[3,128]{1,0:T(4,128)S(1)}, /*index=5*/s32[]{:T(128)}) while((s32[]{:T(128)}, f32[6,3,107]{2,1,0:T(4,128)S(1)}, f32[3,128]{1,0:T(4,128)S(1)}, f32[6,3,107]{2,0,1:T(8,128)S(1)}, f32[3,128]{1,0:T(4,128)S(1)}, ...), condition=%wide.region_19.19_spmd, body=%wide.region_15.18_spmd.sunk | while | flops 479362 | bytes 457577 | solution.py:43
  70.6 2.6 %while.68 = (s32[]{:T(128)}, f32[6,3,107]{2,1,0:T(4,128)S(1)}, f32[3,128]{1,0:T(4,128)S(1)}, f32[6,3,107]{2,0,1:T(8,128)S(1)}, f32[3,128]{1,0:T(4,128)S(1)}, /*index=5*/s32[]{:T(128)}) while((s32[]{:T(128)}, f32[6,3,107]{2,1,0:T(4,128)S(1)}, f32[3,128]{1,0:T(4,128)S(1)}, f32[6,3,107]{2,0,1:T(8,128)S(1)}, f32[3,128]{1,0:T(4,128)S(1)}, ...), condition=%wide.region_19.19_spmd, body=%wide.region_15.18_spmd.sunk | while | flops 479362 | bytes 457577 | solution.py:43
  75.3 2.6 %while.68 = (s32[]{:T(128)}, f32[6,3,107]{2,1,0:T(4,128)S(1)}, f32[3,128]{1,0:T(4,128)S(1)}, f32[6,3,107]{2,0,1:T(8,128)S(1)}, f32[3,128]{1,0:T(4,128)S(1)}, /*index=5*/s32[]{:T(128)}) while((s32[]{:T(128)}, f32[6,3,107]{2,1,0:T(4,128)S(1)}, f32[3,128]{1,0:T(4,128)S(1)}, f32[6,3,107]{2,0,1:T(8,128)S(1)}, f32[3,128]{1,0:T(4,128)S(1)}, ...), condition=%wide.region_19.19_spmd, body=%wide.region_15.18_spmd.sunk | while | flops 479362 | bytes 457577 | solution.py:43
  80.0 2.6 %while.68 = (s32[]{:T(128)}, f32[6,3,107]{2,1,0:T(4,128)S(1)}, f32[3,128]{1,0:T(4,128)S(1)}, f32[6,3,107]{2,0,1:T(8,128)S(1)}, f32[3,128]{1,0:T(4,128)S(1)}, /*index=5*/s32[]{:T(128)}) while((s32[]{:T(128)}, f32[6,3,107]{2,1,0:T(4,128)S(1)}, f32[3,128]{1,0:T(4,128)S(1)}, f32[6,3,107]{2,0,1:T(8,128)S(1)}, f32[3,128]{1,0:T(4,128)S(1)}, ...), condition=%wide.region_19.19_spmd, body=%wide.region_15.18_spmd.sunk | while | flops 479362 | bytes 457577 | solution.py:43
  84.8 2.6 %while.68 = (s32[]{:T(128)}, f32[6,3,107]{2,1,0:T(4,128)S(1)}, f32[3,128]{1,0:T(4,128)S(1)}, f32[6,3,107]{2,0,1:T(8,128)S(1)}, f32[3,128]{1,0:T(4,128)S(1)}, /*index=5*/s32[]{:T(128)}) while((s32[]{:T(128)}, f32[6,3,107]{2,1,0:T(4,128)S(1)}, f32[3,128]{1,0:T(4,128)S(1)}, f32[6,3,107]{2,0,1:T(8,128)S(1)}, f32[3,128]{1,0:T(4,128)S(1)}, ...), condition=%wide.region_19.19_spmd, body=%wide.region_15.18_spmd.sunk | while | flops 479362 | bytes 457577 | solution.py:43
  88.1 1.5 bitcast_reduce_fusion
  94.8 1.3 fusion.19
  98.9 2.2 %gather_fusion.1 = bf16[2,3,2562]{2,1,0:T(4,128)(2,1)} fusion(bf16[8,3,2562]{2,1,0:T(4,128)(2,1)} %copy.76, s32[1024]{0:T(1024)} %pad_clamp_fusion.3), kind=kCustom, calls=%fused_computation.1 | custom fusion | bytes 61496 | tf_op jit(solution)/shard_map/gather | solution.py:91
  101.2 2.2 %gather_fusion.2 = bf16[2,3,2562]{2,1,0:T(4,128)(2,1)} fusion(bf16[8,3,2562]{2,1,0:T(4,128)(2,1)} %copy.77, s32[1024]{0:T(1024)} %pad_clamp_fusion.3), kind=kCustom, calls=%fused_computation.2 | custom fusion | bytes 61496 | tf_op jit(solution)/shard_map/gather | solution.py:91
  103.4 47.6 %while.61 = (s32[]{:T(128)}, f32[2,3,642]{2,0,1:T(2,128)}, bf16[2,3,642]{2,1,0:T(4,128)(2,1)}, bf16[2,3,2562]{2,1,0:T(4,128)(2,1)}, bf16[2,3,2562]{2,1,0:T(4,128...) while((s32[]{:T(128)}, f32[2,3,642]{2,0,1:T(2,128)}, bf16[2,3,642]{2,1,0:T(4,128)(2,1)}, ...), condition=%wide.region_6.7_spmd, body=%wide.region_0.6_spmd.sunk | while | flops 9619678 | bytes 9207262 | solution.py:91
  104.2 1.4 bitcast_convert_fusion.6
  106.3 19.4 %while.66 = (s32[]{:T(128)}, f32[6,3,107]{2,1,0:T(4,128)S(1)}, f32[3,2562]{1,0:T(4,128)S(1)}, f32[6,3,107]{2,0,1:T(8,128)S(1)}, f32[3,2562]{1,0:T(4,128)}, /*index=5*/s32[]{:T(128)}) while((s32[]{:T(128)}, f32[6,3,107]{2,1,0:T(4,128)S(1)}, f32[3,2562]{1,0:T(4,128)S(1)}, f32[6,3,107]{2,0,1:T(8,128)S(1)}, f32[3,2562]{1,0:T(4,128)}, ...), condition=%wide.region_5.5_spmd, body=%wide.region_1.4_spmd.sunk | while | flops 9594692 | bytes 9031429 | solution.py:43
  106.3 1.9 fusion.64
  109.6 1.9 fusion.64
  112.8 1.9 fusion.64
  116.1 1.9 fusion.64
  119.3 1.9 fusion.64
  122.5 1.9 fusion.64
  125.8 1.4 dynamic_update_slice.33
  128.0 1.4 bitcast_convert_fusion.6
  130.1 19.4 %while.66 = (s32[]{:T(128)}, f32[6,3,107]{2,1,0:T(4,128)S(1)}, f32[3,2562]{1,0:T(4,128)S(1)}, f32[6,3,107]{2,0,1:T(8,128)S(1)}, f32[3,2562]{1,0:T(4,128)}, /*index=5*/s32[]{:T(128)}) while((s32[]{:T(128)}, f32[6,3,107]{2,1,0:T(4,128)S(1)}, f32[3,2562]{1,0:T(4,128)S(1)}, f32[6,3,107]{2,0,1:T(8,128)S(1)}, f32[3,2562]{1,0:T(4,128)}, ...), condition=%wide.region_5.5_spmd, body=%wide.region_1.4_spmd.sunk | while | flops 9594692 | bytes 9031429 | solution.py:43
  130.1 1.9 fusion.64
  133.4 1.9 fusion.64
  136.6 1.9 fusion.64
  139.9 1.9 fusion.64
  143.1 1.9 fusion.64
  146.3 1.9 fusion.64
  149.6 1.4 dynamic_update_slice.33
  151.0 4.1 %all-to-all-start.1 = ((bf16[4,3,642]{2,1,0:T(4,128)(2,1)}), bf16[4,3,642]{2,1,0:T(4,128)(2,1)}, u32[]{:S(2)}, u32[]{:S(2)}) async-start(bf16[4,3,642]{2,1,0:T(4,128)(2,1)} %gather_fusion.5), calls=%async_computation.1 | async-start | bytes 49152 | tf_op jit(solution)/shard_map/all_to_all | solution.py:96
  155.2 1.6 fusion.40
  156.8 3.2 %all-to-all-done.1 = bf16[4,3,642]{2,1,0:T(4,128)(2,1)} async-done(((bf16[4,3,642]{2,1,0:T(4,128)(2,1)}), bf16[4,3,642]{2,1,0:T(4,128)(2,1)}, u32[]{:S(2)}, u32[]{:S(2)}) %all-to-all-start.1) | async-done | bytes 15440 | tf_op jit(solution)/shard_map/all_to_all | solution.py:96
  160.0 43.1 %while.63 = (s32[]{:T(128)}, f32[4,3,642]{2,1,0:T(4,128)}, bf16[4,3,642]{2,1,0:T(4,128)(2,1)}, bf16[4,3,642]{2,1,0:T(4,128)(2,1)}, bf16[4,3,642]{2,1,0:T(4,128)(...) while((s32[]{:T(128)}, f32[4,3,642]{2,1,0:T(4,128)}, bf16[4,3,642]{2,1,0:T(4,128)(2,1)}, ...), condition=%wide.region_13.14_spmd, body=%wide.region_7.13_spmd.sunk | while | flops 2411998 | bytes 2346310 | solution.py:111
  162.2 7.9 %while.67 = (s32[]{:T(128)}, f32[6,3,107]{2,1,0:T(4,128)S(1)}, f32[3,642]{1,0:T(4,128)S(1)}, f32[6,3,107]{2,0,1:T(8,128)S(1)}, f32[3,642]{1,0:T(4,128)S(1)}, /*index=5*/s32[]{:T(128)}) while((s32[]{:T(128)}, f32[6,3,107]{2,1,0:T(4,128)S(1)}, f32[3,642]{1,0:T(4,128)S(1)}, f32[6,3,107]{2,0,1:T(8,128)S(1)}, f32[3,642]{1,0:T(4,128)S(1)}, ...), condition=%wide.region_12.12_spmd, body=%wide.region_8.11_spmd.sunk | while | flops 2404292 | bytes 2242185 | solution.py:43
  173.0 7.9 %while.67 = (s32[]{:T(128)}, f32[6,3,107]{2,1,0:T(4,128)S(1)}, f32[3,642]{1,0:T(4,128)S(1)}, f32[6,3,107]{2,0,1:T(8,128)S(1)}, f32[3,642]{1,0:T(4,128)S(1)}, /*index=5*/s32[]{:T(128)}) while((s32[]{:T(128)}, f32[6,3,107]{2,1,0:T(4,128)S(1)}, f32[3,642]{1,0:T(4,128)S(1)}, f32[6,3,107]{2,0,1:T(8,128)S(1)}, f32[3,642]{1,0:T(4,128)S(1)}, ...), condition=%wide.region_12.12_spmd, body=%wide.region_8.11_spmd.sunk | while | flops 2404292 | bytes 2242185 | solution.py:43
  183.7 7.9 %while.67 = (s32[]{:T(128)}, f32[6,3,107]{2,1,0:T(4,128)S(1)}, f32[3,642]{1,0:T(4,128)S(1)}, f32[6,3,107]{2,0,1:T(8,128)S(1)}, f32[3,642]{1,0:T(4,128)S(1)}, /*index=5*/s32[]{:T(128)}) while((s32[]{:T(128)}, f32[6,3,107]{2,1,0:T(4,128)S(1)}, f32[3,642]{1,0:T(4,128)S(1)}, f32[6,3,107]{2,0,1:T(8,128)S(1)}, f32[3,642]{1,0:T(4,128)S(1)}, ...), condition=%wide.region_12.12_spmd, body=%wide.region_8.11_spmd.sunk | while | flops 2404292 | bytes 2242185 | solution.py:43
  194.5 7.9 %while.67 = (s32[]{:T(128)}, f32[6,3,107]{2,1,0:T(4,128)S(1)}, f32[3,642]{1,0:T(4,128)S(1)}, f32[6,3,107]{2,0,1:T(8,128)S(1)}, f32[3,642]{1,0:T(4,128)S(1)}, /*index=5*/s32[]{:T(128)}) while((s32[]{:T(128)}, f32[6,3,107]{2,1,0:T(4,128)S(1)}, f32[3,642]{1,0:T(4,128)S(1)}, f32[6,3,107]{2,0,1:T(8,128)S(1)}, f32[3,642]{1,0:T(4,128)S(1)}, ...), condition=%wide.region_12.12_spmd, body=%wide.region_8.11_spmd.sunk | while | flops 2404292 | bytes 2242185 | solution.py:43
  204.0 1.6 fusion.26
  (670 shorter events, 117.1 us)
Async XLA Ops:
  0.0 94.8 %copy-start = (bf16[642,2562]{1,0:T(8,128)(2,1)S(1)}, bf16[642,2562]{1,0:T(8,128)(2,1)}, u32[]{:S(2)}) copy-start(bf16[642,2562]{1,0:T(8,128)(2,1)} %param.26) | copy-start | bytes 9868828
  1.5 93.3 %collective-permute-start = (bf16[2,3,642]{2,0,1:T(2,128)(2,1)}, bf16[2,3,642]{2,0,1:T(2,128)(2,1)}, u32[]{:S(2)}, u32[]{:S(2)}) collective-permute-start(bf16[2,3,642]{2,0,1:T(2,128)(2,1)} %get-tuple-element.324), channel_id=1, source_target_pairs={{0,1},{1,2},{2,3},{3,4},{4,5},{5,6},{6,7},{8,9},{9,10},{10,11},{11... | collective-permute-start | bytes 23120 | tf_op jit(solution)/shard_map/ppermute | solution.py:20
  4.5 90.3 %collective-permute-start.1 = (bf16[2,3,642]{2,0,1:T(2,128)(2,1)}, bf16[2,3,642]{2,0,1:T(2,128)(2,1)}, u32[]{:S(2)}, u32[]{:S(2)}) collective-permute-start(bf16[2,3,642]{2,0,1:T(2,128)(2,1)} %get-tuple-element.325), channel_id=1, source_target_pairs={{1,0},{2,1},{3,2},{4,3},{5,4},{6,5},{7,6},{9,8},{10,9},{11,10},{12... | collective-permute-start | bytes 23120 | tf_op jit(solution)/shard_map/ppermute | solution.py:23
  7.2 89.7 %collective-permute-start.2 = (bf16[2,3,642]{2,0,1:T(2,128)(2,1)}, bf16[2,3,642]{2,0,1:T(2,128)(2,1)}, u32[]{:S(2)}, u32[]{:S(2)}) collective-permute-start(bf16[2,3,642]{2,0,1:T(2,128)(2,1)} %get-tuple-element.322), channel_id=1, source_target_pairs={{0,1},{1,2},{2,3},{3,4},{4,5},{5,6},{6,7},{8,9},{9,10},{10,11},{11... | collective-permute-start | bytes 23120 | tf_op jit(solution)/shard_map/ppermute | solution.py:20
  12.4 84.4 %collective-permute-start.3 = (bf16[2,3,642]{2,0,1:T(2,128)(2,1)}, bf16[2,3,642]{2,0,1:T(2,128)(2,1)}, u32[]{:S(2)}, u32[]{:S(2)}) collective-permute-start(bf16[2,3,642]{2,0,1:T(2,128)(2,1)} %get-tuple-element.323), channel_id=1, source_target_pairs={{1,0},{2,1},{3,2},{4,3},{5,4},{6,5},{7,6},{9,8},{10,9},{11,10},{12... | collective-permute-start | bytes 23120 | tf_op jit(solution)/shard_map/ppermute | solution.py:23
  15.1 8.8 %copy-start.3 = (s32[1024]{0:T(1024)}, s32[1024]{0:T(1024)S(1)}, u32[]{:S(2)}) copy-start(s32[1024]{0:T(1024)S(1)} %pad_clamp_fusion.1) | copy-start | bytes 12292
  16.3 134.7 %all-to-all-start = ((bf16[4,3,642]{2,1,0:T(4,128)(2,1)}), bf16[4,3,642]{2,1,0:T(4,128)(2,1)}, u32[]{:S(2)}, u32[]{:S(2)}) async-start(bf16[4,3,642]{2,1,0:T(4,128)(2,1)} %gather_fusion.4), calls=%async_computation | async-start | bytes 49152 | tf_op jit(solution)/shard_map/all_to_all | solution.py:95
  88.1 8.8 %copy-start.2 = (bf16[1,4,3,642]{3,1,2,0:T(4,128)(2,1)S(1)}, bf16[1,4,3,642]{3,1,2,0:T(4,128)(2,1)}, u32[]{:S(2)}) copy-start(bf16[1,4,3,642]{3,1,2,0:T(4,128)(2,1)} %param.25) | copy-start | bytes 46228
  106.3 2.1 %copy-start.1 = (f32[3,2562]{1,0:T(4,128)S(1)}, f32[3,2562]{1,0:T(4,128)}, u32[]{:S(2)}) copy-start(f32[3,2562]{1,0:T(4,128)} %get-tuple-element.639) | copy-start | bytes 92236 | tf_op jit(solution)/shard_map/while/body/eval_jaxpr/while
  109.5 2.1 %copy-start.1 = (f32[3,2562]{1,0:T(4,128)S(1)}, f32[3,2562]{1,0:T(4,128)}, u32[]{:S(2)}) copy-start(f32[3,2562]{1,0:T(4,128)} %get-tuple-element.639) | copy-start | bytes 92236 | tf_op jit(solution)/shard_map/while/body/eval_jaxpr/while
  112.8 2.1 %copy-start.1 = (f32[3,2562]{1,0:T(4,128)S(1)}, f32[3,2562]{1,0:T(4,128)}, u32[]{:S(2)}) copy-start(f32[3,2562]{1,0:T(4,128)} %get-tuple-element.639) | copy-start | bytes 92236 | tf_op jit(solution)/shard_map/while/body/eval_jaxpr/while
  116.0 2.1 %copy-start.1 = (f32[3,2562]{1,0:T(4,128)S(1)}, f32[3,2562]{1,0:T(4,128)}, u32[]{:S(2)}) copy-start(f32[3,2562]{1,0:T(4,128)} %get-tuple-element.639) | copy-start | bytes 92236 | tf_op jit(solution)/shard_map/while/body/eval_jaxpr/while
  119.3 2.1 %copy-start.1 = (f32[3,2562]{1,0:T(4,128)S(1)}, f32[3,2562]{1,0:T(4,128)}, u32[]{:S(2)}) copy-start(f32[3,2562]{1,0:T(4,128)} %get-tuple-element.639) | copy-start | bytes 92236 | tf_op jit(solution)/shard_map/while/body/eval_jaxpr/while
  122.5 2.1 %copy-start.1 = (f32[3,2562]{1,0:T(4,128)S(1)}, f32[3,2562]{1,0:T(4,128)}, u32[]{:S(2)}) copy-start(f32[3,2562]{1,0:T(4,128)} %get-tuple-element.639) | copy-start | bytes 92236 | tf_op jit(solution)/shard_map/while/body/eval_jaxpr/while
  130.1 2.1 %copy-start.1 = (f32[3,2562]{1,0:T(4,128)S(1)}, f32[3,2562]{1,0:T(4,128)}, u32[]{:S(2)}) copy-start(f32[3,2562]{1,0:T(4,128)} %get-tuple-element.639) | copy-start | bytes 92236 | tf_op jit(solution)/shard_map/while/body/eval_jaxpr/while
  133.3 2.1 %copy-start.1 = (f32[3,2562]{1,0:T(4,128)S(1)}, f32[3,2562]{1,0:T(4,128)}, u32[]{:S(2)}) copy-start(f32[3,2562]{1,0:T(4,128)} %get-tuple-element.639) | copy-start | bytes 92236 | tf_op jit(solution)/shard_map/while/body/eval_jaxpr/while
  136.6 2.1 %copy-start.1 = (f32[3,2562]{1,0:T(4,128)S(1)}, f32[3,2562]{1,0:T(4,128)}, u32[]{:S(2)}) copy-start(f32[3,2562]{1,0:T(4,128)} %get-tuple-element.639) | copy-start | bytes 92236 | tf_op jit(solution)/shard_map/while/body/eval_jaxpr/while
  139.8 2.1 %copy-start.1 = (f32[3,2562]{1,0:T(4,128)S(1)}, f32[3,2562]{1,0:T(4,128)}, u32[]{:S(2)}) copy-start(f32[3,2562]{1,0:T(4,128)} %get-tuple-element.639) | copy-start | bytes 92236 | tf_op jit(solution)/shard_map/while/body/eval_jaxpr/while
  143.1 2.1 %copy-start.1 = (f32[3,2562]{1,0:T(4,128)S(1)}, f32[3,2562]{1,0:T(4,128)}, u32[]{:S(2)}) copy-start(f32[3,2562]{1,0:T(4,128)} %get-tuple-element.639) | copy-start | bytes 92236 | tf_op jit(solution)/shard_map/while/body/eval_jaxpr/while
  146.3 2.1 %copy-start.1 = (f32[3,2562]{1,0:T(4,128)S(1)}, f32[3,2562]{1,0:T(4,128)}, u32[]{:S(2)}) copy-start(f32[3,2562]{1,0:T(4,128)} %get-tuple-element.639) | copy-start | bytes 92236 | tf_op jit(solution)/shard_map/while/body/eval_jaxpr/while
  151.0 9.0 %all-to-all-start.1 = ((bf16[4,3,642]{2,1,0:T(4,128)(2,1)}), bf16[4,3,642]{2,1,0:T(4,128)(2,1)}, u32[]{:S(2)}, u32[]{:S(2)}) async-start(bf16[4,3,642]{2,1,0:T(4,128)(2,1)} %gather_fusion.5), calls=%async_computation.1 | async-start | bytes 49152 | tf_op jit(solution)/shard_map/all_to_all | solution.py:96
  160.0 43.1 %copy-start.5 = (f32[4]{0:T(128)S(1)}, f32[4]{0:T(128)}, u32[]{:S(2)}) copy-start(f32[4]{0:T(128)} %compare_convert_fusion) | copy-start | bytes 52
  160.0 44.0 %copy-start.4 = (s32[1,1,4]{2,1,0:T(1,128)S(1)}, s32[1,1,4]{2,1,0:T(1,128)}, u32[]{:S(2)}) copy-start(s32[1,1,4]{2,1,0:T(1,128)} %param.32) | copy-start | bytes 52
where the time goes:
time: 209 us; the launch traced here: 206 us
  other arithmetic  118 us (56%)
  local copies, waits for them, and re-layouts  31.9 us (15%)
  blocking collectives  23 us (11%)
  starting transfers between devices  18.8 us (9%)
  matrix products  5.87 us (3%)
  loops' own time  4.32 us (2%)
  waiting for transfers between devices  3.21 us (2%)
    reduce_sum x84, other arithmetic, kernel_rows(): along_offset = jnp.sum(offset * strength[:, None, :], axis=0)  42 us
    reduce_sum x84, other arithmetic, kernel_rows(): return jnp.sum(summand, axis=2) / (8.0 * math.pi)  37.9 us
    all_gather x1, blocking collectives, local(): lax.all_gather(wall_points[0], 'slab', axis=0, tiled=True)  14.1 us
    transpose x14, other arithmetic, stokes_block(): blocked = targets.reshape(3, 6, points // 6).transpose(1, 0, 2)  9.75 us
    all_gather x1, blocking collectives, local(): lax.all_gather(wall_traction[0], 'slab', axis=0, tiled=True)  8.97 us
    ppermute x2, starting transfers between devices, with_halo(): lax.ppermute(lax.slice_in_dim(block, block.shape[dim] - width, None, axis...  8.21 us
    mul x8, other arithmetic, wall_pair(): source_den.astype(jnp.float32) * WALL_GAIN  5.35 us
    add x84, other arithmetic, kernel_rows(): distance2 + 2.0 * EPSILON2  4.91 us
  transfers between devices with their start and end apart: 6, of which 1 were waited for; matrix products, arithmetic and copies ran while one was open for 54% of the time, Pallas kernels for 0%

commit v1 on v0

v1 whole, which is shorter than its diff:
```python
import functools
import math

import jax
import jax.numpy as jnp
from jax import lax
from jax.experimental import pallas as pl
from jax.experimental.pallas import tpu as pltpu
from jax.sharding import PartitionSpec as P

MESH = pl.DeviceIdType.MESH
HALO = 2
EPSILON2 = 0.05
WALL_GAIN = 3.0
LANES = 128
TERMS = 16
KAPPA = 1.0 / EPSILON2
F32 = jnp.float32
BF16 = jnp.bfloat16


def up(n, m):
    return -(-n // m) * m


def split(value, parts):
    out = []
    for _ in range(parts):
        piece = value.astype(BF16).astype(F32)
        out.append(piece)
        value = value - piece
    return out


def kernel(
    cfg,
    pair_target, pair_source, junction_cell, junction_target, wall_near,
    positions, density, upsample, quad, coarse, wall_points, wall_traction,
    out,
    own, cells, jsend, jrecv, walls, ups, rows, lhs, fine, ysrc, gsrc, yd, yg, ga, gb, xt, acc,
    local_sem, halo_send, halo_recv, junction_send, junction_recv, wall_send, wall_recv,
):
    count, points, fine_points, pairs, near, patch, segs, slabs, per_slab = cfg
    pt, qp = up(points, LANES), up(fine_points, LANES)
    rows_t = up(points, 16)
    seg, slab = lax.axis_index("seg"), lax.axis_index("slab")

    copies = [
        pltpu.make_async_copy(positions.at[0], cells.at[pl.ds(HALO, count), 0], local_sem.at[0]),
        pltpu.make_async_copy(density.at[0], cells.at[pl.ds(HALO, count), 1], local_sem.at[1]),
        pltpu.make_async_copy(wall_points.at[0], walls.at[pl.ds(slab * per_slab, per_slab), 0], local_sem.at[2]),
        pltpu.make_async_copy(wall_traction.at[0], walls.at[pl.ds(slab * per_slab, per_slab), 1], local_sem.at[3]),
    ]
    home = [
        pltpu.make_async_copy(positions.at[0], own.at[0], local_sem.at[5]),
        pltpu.make_async_copy(density.at[0], own.at[1], local_sem.at[6]),
    ]
    big = pltpu.make_async_copy(upsample, ups, local_sem.at[4])
    for copy in home + copies:
        copy.start()
    big.start()

    barrier = pltpu.get_barrier_semaphore()
    for o in range(1, segs):
        pl.semaphore_signal(barrier, inc=1, device_id={"seg": lax.rem(seg + o, segs)}, device_id_type=MESH)
    for o in range(1, slabs):
        pl.semaphore_signal(barrier, inc=1, device_id={"slab": lax.rem(slab + o, slabs)}, device_id_type=MESH)

    for copy in home + copies:
        copy.wait()
    for b in range(segs):
        jsend[b, 0] = own[0, junction_cell[0, 0, b]]
        jsend[b, 1] = own[1, junction_cell[0, 0, b]]
    ysrc[...] = jnp.zeros_like(ysrc)
    gsrc[...] = jnp.zeros_like(gsrc)

    @pl.when(slab == 0)
    def _():
        cells[0:HALO] = jnp.zeros((HALO,) + cells.shape[1:], BF16)

    @pl.when(slab == slabs - 1)
    def _():
        cells[HALO + count:] = jnp.zeros((HALO,) + cells.shape[1:], BF16)

    pl.semaphore_wait(barrier, segs - 1 + slabs - 1)

    def halo_up():
        return pltpu.make_async_remote_copy(
            cells.at[pl.ds(count, HALO)], cells.at[pl.ds(0, HALO)], halo_send.at[0], halo_recv.at[0],
            device_id={"slab": lax.rem(slab + 1, slabs)}, device_id_type=MESH)

    def halo_down():
        return pltpu.make_async_remote_copy(
            cells.at[pl.ds(HALO, HALO)], cells.at[pl.ds(HALO + count, HALO)], halo_send.at[1], halo_recv.at[1],
            device_id={"slab": lax.rem(slab + slabs - 1, slabs)}, device_id_type=MESH)

    def junction(o):
        return pltpu.make_async_remote_copy(
            jsend.at[lax.rem(seg + o, segs)], jrecv.at[seg], junction_send.at[o], junction_recv.at[o],
            device_id={"seg": lax.rem(seg + o, segs)}, device_id_type=MESH)

    def junction_in(o):
        return pltpu.make_async_remote_copy(
            jsend.at[seg], jrecv.at[lax.rem(seg + segs - o, segs)], junction_send.at[o], junction_recv.at[o],
            device_id={"seg": lax.rem(seg + o, segs)}, device_id_type=MESH)

    def wall(o, of):
        slot = pl.ds(of * per_slab, per_slab)
        return pltpu.make_async_remote_copy(
            walls.at[slot], walls.at[slot], wall_send.at[o], wall_recv.at[o],
            device_id={"slab": lax.rem(slab + o, slabs)}, device_id_type=MESH)

    @pl.when(slab < slabs - 1)
    def _():
        halo_up().start()

    @pl.when(slab > 0)
    def _():
        halo_down().start()

    for o in range(1, segs):
        junction(o).start()
    for o in range(slabs - 1, 0, -1):
        wall(o, slab).start()

    rows[...] = jnp.zeros_like(rows)
    for c in range(count):
        x = own[0, c].astype(F32)
        rows[0:3, 0:points] = x
        rows[3:6, 0:points] = x
        for i, piece in enumerate(split(KAPPA * jnp.sum(x * x, axis=0, keepdims=True), 3)):
            rows[6 + i:7 + i, 0:points] = piece
        rows[9:12, 0:points] = jnp.ones((3, points), F32)
        xt[c] = rows[...].T[0:rows_t].astype(BF16)
        acc[c] = jnp.zeros(acc.shape[1:], F32)

    def prepare(start, size):
        at = pl.ds(start, size)
        y, g = ysrc[0:3, at], gsrc[0:3, at]
        g_hi, g_lo = split(g, 2)
        y_hi, y_lo = split((-2.0 * KAPPA) * y, 2)
        norm = split(KAPPA * jnp.sum(y * y, axis=0, keepdims=True) + 1.0, 3)
        dot = split(-jnp.sum(y * (g_hi + g_lo), axis=0, keepdims=True), 3)
        one = jnp.ones((3, size), F32)
        none = jnp.zeros((3, size), F32)
        pad = jnp.zeros((TERMS - 12, size), F32)
        yd[:, at] = jnp.concatenate([y_hi, y_lo, one] + norm + [pad], axis=0).astype(BF16)
        yg[:, at] = jnp.concatenate([g_hi, g_lo, none] + dot + [pad], axis=0).astype(BF16)
        ga[:, at] = jnp.concatenate([one[0:1], y, jnp.zeros((TERMS - 4, size), F32)], axis=0).astype(BF16)
        gb[:, at] = jnp.concatenate([jnp.zeros((TERMS - 8, size), F32), g_hi, g_lo, none[0:2]], axis=0).astype(BF16)

    def chunk(targets, start):
        at = pl.ds(pl.multiple_of(start, LANES), LANES)
        first = jnp.dot(
            targets, jnp.concatenate([yd[:, at], yg[:, at]], axis=1), preferred_element_type=F32)
        inverse = lax.rsqrt(first[:, :LANES])
        inverse3 = inverse * inverse * inverse
        along = (first[:, LANES:] * inverse3).astype(BF16)
        plain = (inverse + inverse3).astype(BF16)
        return lax.dot_general(
            jnp.concatenate([ga[:, at], gb[:, at]], axis=1),
            jnp.concatenate([along, plain], axis=1),
            (((1,), (1,)), ((), ())), preferred_element_type=F32)

    def block(target, start, chunks):
        targets = xt[target]
        unroll = 3 if chunks % 3 == 0 else (2 if chunks % 2 == 0 else 1)

        def step(i, total):
            for u in range(unroll):
                total = total + chunk(targets, start + (i * unroll + u) * LANES)
            return total

        zero = jnp.zeros((TERMS, rows_t), F32)
        if chunks == unroll:
            return step(0, zero)
        return lax.fori_loop(0, chunks // unroll, step, zero)

    def add(target, value):
        for c in range(count):
            acc[c] = acc[c] + jnp.where(target == c, 1.0, 0.0) * value

    @pl.when(slab > 0)
    def _():
        halo_up().wait_recv()

    @pl.when(slab < slabs - 1)
    def _():
        halo_down().wait_recv()

    for k in range(pairs):
        source = cells[pair_source[0, k]]
        lhs[6 * k:6 * k + 3] = source[0].astype(F32)
        lhs[6 * k + 3:6 * k + 6] = source[1].astype(F32)
    big.wait()
    fine[...] = jnp.dot(lhs[...].astype(BF16), ups[...], preferred_element_type=F32).astype(BF16).astype(F32)
    for k in range(pairs):
        ysrc[0:3, pl.ds(k * qp, fine_points)] = fine[6 * k:6 * k + 3]
        gsrc[0:3, pl.ds(k * qp, fine_points)] = fine[6 * k + 3:6 * k + 6] * quad[...]
    prepare(0, pairs * qp)
    for k in range(pairs):
        target = pair_target[0, k]
        add(target, block(target, k * qp, qp // LANES))

    base = pairs * qp
    for o in range(1, segs):
        junction_in(o).wait_recv()
        source = jrecv[lax.rem(seg + segs - o, segs)]
        at = pl.ds(base + (o - 1) * pt, points)
        ysrc[0:3, at] = source[0].astype(F32)
        gsrc[0:3, at] = source[1].astype(F32) * coarse[...]
    prepare(base, (segs - 1) * pt)
    for o in range(1, segs):
        target = junction_target[0, 0, lax.rem(seg + segs - o, segs)]
        add(target, block(target, base + (o - 1) * pt, pt // LANES))

    base = base + (segs - 1) * pt
    for o in range(1, slabs):
        wall(o, lax.rem(slab + slabs - o, slabs)).wait_recv()
    width = up(patch, LANES)
    for c in range(count):
        for n in range(near):
            source = walls[wall_near[0, c, n]]
            at = pl.ds(base + (c * near + n) * width, patch)
            ysrc[0:3, at] = source[0].astype(F32)
            gsrc[0:3, at] = source[1].astype(F32) * WALL_GAIN
    prepare(base, count * near * width)
    scale = 1.0 / (math.sqrt(EPSILON2) * 8.0 * math.pi)
    for c in range(count):
        total = (acc[c] + block(c, base + c * near * width, near * width // LANES))[:, 0:points]
        x = own[0, c].astype(F32)
        out[0, c] = scale * (total[8:11] + total[11:14] + KAPPA * (x * total[0:1] - total[1:4]))

    @pl.when(slab < slabs - 1)
    def _():
        halo_up().wait_send()

    @pl.when(slab > 0)
    def _():
        halo_down().wait_send()

    for o in range(1, segs):
        junction(o).wait_send()
    for o in range(1, slabs):
        wall(o, slab).wait_send()


def local(segs, slabs, positions, density, upsample, quad_weights, coarse_weights, pair_target, pair_source,
          junction_cell, junction_target, wall_points, wall_traction, wall_near):
    count, points = positions.shape[1], positions.shape[3]
    fine_points = upsample.shape[1]
    pairs, near = pair_target.shape[1], wall_near.shape[2]
    per_slab, patch = wall_points.shape[1], wall_points.shape[3]
    cfg = (count, points, fine_points, pairs, near, patch, segs, slabs, per_slab)
    pt, qp = up(points, LANES), up(fine_points, LANES)
    lanes = pairs * qp + (segs - 1) * pt + count * near * up(patch, LANES)
    smem = pl.BlockSpec(memory_space=pltpu.SMEM)
    vmem = pl.BlockSpec(memory_space=pltpu.VMEM)
    far = pl.BlockSpec(memory_space=pl.ANY)
    dma = pltpu.SemaphoreType.DMA
    return pl.pallas_call(
        functools.partial(kernel, cfg),
        out_shape=jax.ShapeDtypeStruct(positions.shape, F32),
        in_specs=[smem] * 5 + [far, far, far, vmem, vmem, far, far],
        out_specs=vmem,
        scratch_shapes=[
            pltpu.VMEM((2,) + positions.shape[1:], BF16),
            pltpu.VMEM((count + 2 * HALO, 2, 3, points), BF16),
            pltpu.VMEM((segs, 2, 3, points), BF16),
            pltpu.VMEM((segs, 2, 3, points), BF16),
            pltpu.VMEM((slabs * per_slab, 2, 3, patch), BF16),
            pltpu.VMEM(upsample.shape, BF16),
            pltpu.VMEM((TERMS, pt), F32),
            pltpu.VMEM((6 * pairs, points), F32),
            pltpu.VMEM((6 * pairs, fine_points), F32),
            pltpu.VMEM((8, lanes), F32),
            pltpu.VMEM((8, lanes), F32),
            pltpu.VMEM((TERMS, lanes), BF16),
            pltpu.VMEM((TERMS, lanes), BF16),
            pltpu.VMEM((TERMS, lanes), BF16),
            pltpu.VMEM((TERMS, lanes), BF16),
            pltpu.VMEM((count, up(points, 16), TERMS), BF16),
            pltpu.VMEM((count, TERMS, up(points, 16)), F32),
            dma((7,)), dma((2,)), dma((2,)), dma((segs,)), dma((segs,)), dma((slabs,)), dma((slabs,)),
        ],
        compiler_params=pltpu.CompilerParams(collective_id=0, has_side_effects=True),
    )(pair_target, pair_source, junction_cell, junction_target, wall_near,
      positions, density, upsample, quad_weights[None], coarse_weights[None], wall_points, wall_traction)


def solution(mesh):
    placed = (
        P("seg", "slab", None, None),
        P("seg", "slab", None, None),
        P(),
        P(),
        P(),
        P("seg", "slab"),
        P("seg", "slab"),
        P("seg", "slab", None),
        P("seg", "slab", None),
        P("seg", "slab", None, None),
        P("seg", "slab", None, None),
        P("seg", "slab", None),
    )
    body = functools.partial(local, mesh.shape["seg"], mesh.shape["slab"])
    return jax.shard_map(
        body, mesh=mesh, in_specs=placed, out_specs=P("seg", "slab", None, None), check_vma=False
    )
```

time: 209 us -> 35.6 us (0.17)
  the two profiles are of different devices: /device:TPU:0 before, /device:TPU:1 now
where the time goes in v1:
time: 35.6 us; the launch traced here: 35.2 us
  Pallas kernels  27.2 us (76%)
  local copies, waits for them, and re-layouts  8.05 us (23%)
    pallas_call x1, Pallas kernels, local(): pl.pallas_call(functools.partial(kernel, cfg), out_shape=jax.ShapeDtypeSt...  27.2 us
    unnamed x3, local copies, waits for them, and re-layouts  4.03 us
    pallas_call x1, local copies, waits for them, and re-layouts, local(): pl.pallas_call(functools.partial(kernel, cfg), out_shape=jax.ShapeDtypeSt...  1.42 us
    broadcast_in_dim x1, local copies, waits for them, and re-layouts, local(): quad_weights[None]  1.31 us
    broadcast_in_dim x1, local copies, waits for them, and re-layouts, local(): coarse_weights[None]  1.28 us

profile of v1, /device:TPU:1, one launch (start us, length us, event | category | flops | bytes accessed | tf_op | source)
XLA Modules:
  0.0 35.2 jit_solution(3411564513932165066)
XLA Ops:
  0.0 1.4 %copy.13.wall_near = s32[1,4,2]{2,1,0:T(4,128)} copy(s32[1,4,2]{1,2,0:T(2,128)} %param.23) | data formatting | bytes 64 | tf_op args[11]
  1.4 1.3 %broadcast_in_dim.7.coarse = f32[1,642]{1,0:T(1,128)} reshape(f32[642]{0:T(1024)} %param.16) | data formatting | bytes 5136 | tf_op jit(solution)/shard_map/broadcast_in_dim | solution.py:288
  2.6 1.3 %broadcast_in_dim.6.quad = f32[1,2562]{1,0:T(1,128)} reshape(f32[2562]{0:T(1024)} %param.15) | data formatting | bytes 20496 | tf_op jit(solution)/shard_map/broadcast_in_dim | solution.py:288
  3.9 1.3 %copy.14.positions = bf16[1,4,3,642]{3,2,1,0:T(4,128)(2,1)} copy(bf16[1,4,3,642]{3,1,2,0:T(4,128)(2,1)} %param.12) | data formatting | bytes 30816 | tf_op args[0]
  5.3 1.3 %copy.15.density = bf16[1,4,3,642]{3,2,1,0:T(4,128)(2,1)} copy(bf16[1,4,3,642]{3,1,2,0:T(4,128)(2,1)} %param.13) | data formatting | bytes 30816 | tf_op args[1]
  6.6 27.2 %shard_map.118 = f32[1,4,3,642]{3,2,1,0:T(4,128)} custom-call(s32[1,2]{1,0:T(1,128)} %pair_target.1, s32[1,2]{1,0:T(1,128)} %pair_source.1, s32[1,1,4]{2,1,0:T(1,128)} %junction_cell.1, s32[1,1,4]{2,1,0:T(1,128)} %junction_target.1, s32[1,4,2]{2,1,0:T(4,128)} %copy.13.wall_near, bf16[1,4,3,642]{3,2,1,0:T(4,128)(2,1)} %copy.14.positions, ...), custom_call_target="tpu_custom_call" | custom-call | tf_op jit(solution)/shard_map/pallas_call | solution.py:261
  33.8 1.4 %copy.16 = f32[1,4,3,642]{3,1,2,0:T(4,128)} copy(f32[1,4,3,642]{3,2,1,0:T(4,128)} %shard_map.118) | data formatting | bytes 61632 | tf_op jit(solution)/shard_map/pallas_call | solution.py:261

commit v2 on v1

--- a/solution.py
+++ b/solution.py
@@ -37,7 +37,7 @@
     pair_target, pair_source, junction_cell, junction_target, wall_near,
     positions, density, upsample, quad, coarse, wall_points, wall_traction,
     out,
-    own, cells, jsend, jrecv, walls, ups, rows, lhs, fine, ysrc, gsrc, yd, yg, ga, gb, xt, acc,
+    own, low, high, jsend, jrecv, walls, ups, rows, lhs, fine, ysrc, gsrc, yd, yg, ga, gb, xt, xs, wide, acc,
     local_sem, halo_send, halo_recv, junction_send, junction_recv, wall_send, wall_recv,
 ):
     count, points, fine_points, pairs, near, patch, segs, slabs, per_slab = cfg
@@ -46,17 +46,13 @@
     seg, slab = lax.axis_index("seg"), lax.axis_index("slab")
 
     copies = [
-        pltpu.make_async_copy(positions.at[0], cells.at[pl.ds(HALO, count), 0], local_sem.at[0]),
-        pltpu.make_async_copy(density.at[0], cells.at[pl.ds(HALO, count), 1], local_sem.at[1]),
+        pltpu.make_async_copy(positions.at[0], own.at[0], local_sem.at[0]),
+        pltpu.make_async_copy(density.at[0], own.at[1], local_sem.at[1]),
         pltpu.make_async_copy(wall_points.at[0], walls.at[pl.ds(slab * per_slab, per_slab), 0], local_sem.at[2]),
         pltpu.make_async_copy(wall_traction.at[0], walls.at[pl.ds(slab * per_slab, per_slab), 1], local_sem.at[3]),
     ]
-    home = [
-        pltpu.make_async_copy(positions.at[0], own.at[0], local_sem.at[5]),
-        pltpu.make_async_copy(density.at[0], own.at[1], local_sem.at[6]),
-    ]
     big = pltpu.make_async_copy(upsample, ups, local_sem.at[4])
-    for copy in home + copies:
+    for copy in copies:
         copy.start()
     big.start()
 
@@ -66,32 +62,41 @@
     for o in range(1, slabs):
         pl.semaphore_signal(barrier, inc=1, device_id={"slab": lax.rem(slab + o, slabs)}, device_id_type=MESH)
 
-    for copy in home + copies:
+    for copy in copies:
         copy.wait()
+    cell_at = lax.broadcasted_iota(jnp.int32, (count, points), 0)
+
+    def pick(kind, i, near_by):
+        total = jnp.zeros((count, points), F32)
+        for ref, first in near_by:
+            total = total + jnp.where(cell_at == first, ref[kind, i].astype(F32), 0.0)
+        return jnp.sum(total, axis=0, keepdims=True)
+
     for b in range(segs):
-        jsend[b, 0] = own[0, junction_cell[0, 0, b]]
-        jsend[b, 1] = own[1, junction_cell[0, 0, b]]
+        mine = junction_cell[0, 0, b]
+        jsend[b] = jnp.concatenate(
+            [pick(kind, i, [(own, mine)]) for kind in range(2) for i in range(3)], axis=0).astype(BF16)
     ysrc[...] = jnp.zeros_like(ysrc)
     gsrc[...] = jnp.zeros_like(gsrc)
 
     @pl.when(slab == 0)
     def _():
-        cells[0:HALO] = jnp.zeros((HALO,) + cells.shape[1:], BF16)
+        low[...] = jnp.zeros_like(low)
 
     @pl.when(slab == slabs - 1)
     def _():
-        cells[HALO + count:] = jnp.zeros((HALO,) + cells.shape[1:], BF16)
+        high[...] = jnp.zeros_like(high)
 
     pl.semaphore_wait(barrier, segs - 1 + slabs - 1)
 
     def halo_up():
         return pltpu.make_async_remote_copy(
-            cells.at[pl.ds(count, HALO)], cells.at[pl.ds(0, HALO)], halo_send.at[0], halo_recv.at[0],
+            own, low, halo_send.at[0], halo_recv.at[0],
             device_id={"slab": lax.rem(slab + 1, slabs)}, device_id_type=MESH)
 
     def halo_down():
         return pltpu.make_async_remote_copy(
-            cells.at[pl.ds(HALO, HALO)], cells.at[pl.ds(HALO + count, HALO)], halo_send.at[1], halo_recv.at[1],
+            own, high, halo_send.at[1], halo_recv.at[1],
             device_id={"slab": lax.rem(slab + slabs - 1, slabs)}, device_id_type=MESH)
 
     def junction(o):
@@ -124,14 +129,20 @@
         wall(o, slab).start()
 
     rows[...] = jnp.zeros_like(rows)
+    coords = [own[0, i].astype(F32) for i in range(3)]
+    norms = split(KAPPA * (coords[0] * coords[0] + coords[1] * coords[1] + coords[2] * coords[2]), 3)
+    rows[9:12, 0:points] = jnp.ones((3, points), F32)
     for c in range(count):
-        x = own[0, c].astype(F32)
-        rows[0:3, 0:points] = x
-        rows[3:6, 0:points] = x
-        for i, piece in enumerate(split(KAPPA * jnp.sum(x * x, axis=0, keepdims=True), 3)):
-            rows[6 + i:7 + i, 0:points] = piece
-        rows[9:12, 0:points] = jnp.ones((3, points), F32)
-        xt[c] = rows[...].T[0:rows_t].astype(BF16)
+        for i in range(3):
+            line = coords[i][c:c + 1]
+            xs[c, i:i + 1] = line
+            rows[i:i + 1, 0:points] = line
+            rows[3 + i:4 + i, 0:points] = line
+            rows[6 + i:7 + i, 0:points] = norms[i][c:c + 1]
+        turned = rows[...].T[0:rows_t]
+        xt[c] = turned.astype(BF16)
+        for i in range(3):
+            wide[c, i] = jnp.broadcast_to(turned[:, i:i + 1], (rows_t, LANES))
         acc[c] = jnp.zeros(acc.shape[1:], F32)
 
     def prepare(start, size):
@@ -140,7 +151,10 @@
         g_hi, g_lo = split(g, 2)
         y_hi, y_lo = split((-2.0 * KAPPA) * y, 2)
         norm = split(KAPPA * jnp.sum(y * y, axis=0, keepdims=True) + 1.0, 3)
-        dot = split(-jnp.sum(y * (g_hi + g_lo), axis=0, keepdims=True), 3)
+        dot = -jnp.sum(y * (g_hi + g_lo), axis=0, keepdims=True)
+        gsrc[0:3, at] = g_hi + g_lo
+        gsrc[3:4, at] = dot
+        dot = split(dot, 3)
         one = jnp.ones((3, size), F32)
         none = jnp.zeros((3, size), F32)
         pad = jnp.zeros((TERMS - 12, size), F32)
@@ -149,32 +163,44 @@
         ga[:, at] = jnp.concatenate([one[0:1], y, jnp.zeros((TERMS - 4, size), F32)], axis=0).astype(BF16)
         gb[:, at] = jnp.concatenate([jnp.zeros((TERMS - 8, size), F32), g_hi, g_lo, none[0:2]], axis=0).astype(BF16)
 
-    def chunk(targets, start):
-        at = pl.ds(pl.multiple_of(start, LANES), LANES)
-        first = jnp.dot(
-            targets, jnp.concatenate([yd[:, at], yg[:, at]], axis=1), preferred_element_type=F32)
-        inverse = lax.rsqrt(first[:, :LANES])
+    def finish(distance, along, at):
+        inverse = lax.rsqrt(distance)
         inverse3 = inverse * inverse * inverse
-        along = (first[:, LANES:] * inverse3).astype(BF16)
-        plain = (inverse + inverse3).astype(BF16)
         return lax.dot_general(
             jnp.concatenate([ga[:, at], gb[:, at]], axis=1),
-            jnp.concatenate([along, plain], axis=1),
+            jnp.concatenate([(along * inverse3).astype(BF16), (inverse + inverse3).astype(BF16)], axis=1),
             (((1,), (1,)), ((), ())), preferred_element_type=F32)
 
+    def group(target, start, size):
+        targets = xt[target]
+        ats = [pl.ds(pl.multiple_of(start + i * LANES, LANES), LANES) for i in range(size)]
+        total = None
+        for i in range(0, size - 1, 2):
+            pair = jnp.dot(
+                targets, jnp.concatenate([yd[:, ats[i]], yd[:, ats[i + 1]]], axis=1), preferred_element_type=F32)
+            for at, distance in ((ats[i], pair[:, :LANES]), (ats[i + 1], pair[:, LANES:])):
+                along = gsrc[3:4, at] + wide[target, 0] * gsrc[0:1, at]
+                along = along + wide[target, 1] * gsrc[1:2, at]
+                along = along + wide[target, 2] * gsrc[2:3, at]
+                term = finish(distance, along, at)
+                total = term if total is None else total + term
+        if size % 2:
+            at = ats[-1]
+            both = jnp.dot(
+                targets, jnp.concatenate([yd[:, at], yg[:, at]], axis=1), preferred_element_type=F32)
+            term = finish(both[:, :LANES], both[:, LANES:], at)
+            total = term if total is None else total + term
+        return total
+
     def block(target, start, chunks):
-        targets = xt[target]
-        unroll = 3 if chunks % 3 == 0 else (2 if chunks % 2 == 0 else 1)
+        size = 3 if chunks % 3 == 0 else (2 if chunks % 2 == 0 else 1)
 
         def step(i, total):
-            for u in range(unroll):
-                total = total + chunk(targets, start + (i * unroll + u) * LANES)
-            return total
-
-        zero = jnp.zeros((TERMS, rows_t), F32)
-        if chunks == unroll:
-            return step(0, zero)
-        return lax.fori_loop(0, chunks // unroll, step, zero)
+            return total + group(target, start + i * size * LANES, size)
+
+        if chunks == size:
+            return group(target, start, size)
+        return lax.fori_loop(0, chunks // size, step, jnp.zeros((TERMS, rows_t), F32))
 
     def add(target, value):
         for c in range(count):
@@ -189,14 +215,16 @@
         halo_down().wait_recv()
 
     for k in range(pairs):
-        source = cells[pair_source[0, k]]
-        lhs[6 * k:6 * k + 3] = source[0].astype(F32)
-        lhs[6 * k + 3:6 * k + 6] = source[1].astype(F32)
+        source = pair_source[0, k]
+        around = [(low, source + (count - HALO)), (own, source - HALO), (high, source - (HALO + count))]
+        for kind in range(2):
+            for i in range(3):
+                lhs[6 * k + 3 * kind + i:6 * k + 3 * kind + i + 1] = pick(kind, i, around)
     big.wait()
     fine[...] = jnp.dot(lhs[...].astype(BF16), ups[...], preferred_element_type=F32).astype(BF16).astype(F32)
     for k in range(pairs):
         ysrc[0:3, pl.ds(k * qp, fine_points)] = fine[6 * k:6 * k + 3]
-        gsrc[0:3, pl.ds(k * qp, fine_points)] = fine[6 * k + 3:6 * k + 6] * quad[...]
+        gsrc[0:3, pl.ds(k * qp, fine_points)] = fine[6 * k + 3:6 * k + 6] * quad[...][None]
     prepare(0, pairs * qp)
     for k in range(pairs):
         target = pair_target[0, k]
@@ -207,8 +235,8 @@
         junction_in(o).wait_recv()
         source = jrecv[lax.rem(seg + segs - o, segs)]
         at = pl.ds(base + (o - 1) * pt, points)
-        ysrc[0:3, at] = source[0].astype(F32)
-        gsrc[0:3, at] = source[1].astype(F32) * coarse[...]
+        ysrc[0:3, at] = source[0:3].astype(F32)
+        gsrc[0:3, at] = source[3:6].astype(F32) * coarse[...][None]
     prepare(base, (segs - 1) * pt)
     for o in range(1, segs):
         target = junction_target[0, 0, lax.rem(seg + segs - o, segs)]
@@ -220,7 +248,7 @@
     width = up(patch, LANES)
     for c in range(count):
         for n in range(near):
-            source = walls[wall_near[0, c, n]]
+            source = walls[wall_near[0, n, c]]
             at = pl.ds(base + (c * near + n) * width, patch)
             ysrc[0:3, at] = source[0].astype(F32)
             gsrc[0:3, at] = source[1].astype(F32) * WALL_GAIN
@@ -228,8 +256,10 @@
     scale = 1.0 / (math.sqrt(EPSILON2) * 8.0 * math.pi)
     for c in range(count):
         total = (acc[c] + block(c, base + c * near * width, near * width // LANES))[:, 0:points]
-        x = own[0, c].astype(F32)
-        out[0, c] = scale * (total[8:11] + total[11:14] + KAPPA * (x * total[0:1] - total[1:4]))
+        x = xs[c, 0:3]
+        value = scale * (total[8:11] + total[11:14] + KAPPA * (x * total[0:1] - total[1:4]))
+        for i in range(3):
+            out[0, i, c:c + 1] = value[i:i + 1]
 
     @pl.when(slab < slabs - 1)
     def _():
@@ -248,6 +278,7 @@
 def local(segs, slabs, positions, density, upsample, quad_weights, coarse_weights, pair_target, pair_source,
           junction_cell, junction_target, wall_points, wall_traction, wall_near):
     count, points = positions.shape[1], positions.shape[3]
+    turned = (1, 3, count, points)
     fine_points = upsample.shape[1]
     pairs, near = pair_target.shape[1], wall_near.shape[2]
     per_slab, patch = wall_points.shape[1], wall_points.shape[3]
@@ -258,16 +289,17 @@
     vmem = pl.BlockSpec(memory_space=pltpu.VMEM)
     far = pl.BlockSpec(memory_space=pl.ANY)
     dma = pltpu.SemaphoreType.DMA
-    return pl.pallas_call(
+    result = pl.pallas_call(
         functools.partial(kernel, cfg),
-        out_shape=jax.ShapeDtypeStruct(positions.shape, F32),
+        out_shape=jax.ShapeDtypeStruct(turned, F32),
         in_specs=[smem] * 5 + [far, far, far, vmem, vmem, far, far],
         out_specs=vmem,
         scratch_shapes=[
-            pltpu.VMEM((2,) + positions.shape[1:], BF16),
-            pltpu.VMEM((count + 2 * HALO, 2, 3, points), BF16),
-            pltpu.VMEM((segs, 2, 3, points), BF16),
-            pltpu.VMEM((segs, 2, 3, points), BF16),
+            pltpu.VMEM((2,) + turned[1:], BF16),
+            pltpu.VMEM((2,) + turned[1:], BF16),
+            pltpu.VMEM((2,) + turned[1:], BF16),
+            pltpu.VMEM((segs, 6, points), BF16),
+            pltpu.VMEM((segs, 6, points), BF16),
             pltpu.VMEM((slabs * per_slab, 2, 3, patch), BF16),
             pltpu.VMEM(upsample.shape, BF16),
             pltpu.VMEM((TERMS, pt), F32),
@@ -280,12 +312,16 @@
             pltpu.VMEM((TERMS, lanes), BF16),
             pltpu.VMEM((TERMS, lanes), BF16),
             pltpu.VMEM((count, up(points, 16), TERMS), BF16),
+            pltpu.VMEM((count, 3, points), F32),
+            pltpu.VMEM((count, 3, up(points, 16), LANES), F32),
             pltpu.VMEM((count, TERMS, up(points, 16)), F32),
-            dma((7,)), dma((2,)), dma((2,)), dma((segs,)), dma((segs,)), dma((slabs,)), dma((slabs,)),
+            dma((5,)), dma((2,)), dma((2,)), dma((segs,)), dma((segs,)), dma((slabs,)), dma((slabs,)),
         ],
         compiler_params=pltpu.CompilerParams(collective_id=0, has_side_effects=True),
-    )(pair_target, pair_source, junction_cell, junction_target, wall_near,
-      positions, density, upsample, quad_weights[None], coarse_weights[None], wall_points, wall_traction)
+    )(pair_target, pair_source, junction_cell, junction_target, wall_near.transpose(0, 2, 1),
+      positions.transpose(0, 2, 1, 3), density.transpose(0, 2, 1, 3), upsample, quad_weights, coarse_weights,
+      wall_points, wall_traction)
+    return result.transpose(0, 2, 1, 3)
 
 
 def solution(mesh):

time: 35.6 us -> 28.1 us (0.79)
  local copies, waits for them, and re-layouts: 8.05 us -> 1.39 us
  Pallas kernels: 27.2 us -> 26.5 us
    unnamed x3 -> x1, local copies, waits for them, and re-layouts: 4.03 us -> 1.39 us
    broadcast_in_dim x2 -> x0, local copies, waits for them, and re-layouts: 2.59 us -> none  [the longest x1 1.31 us: local(): quad_weights[None]]
    pallas_call x1 -> x0, local copies, waits for them, and re-layouts: 1.42 us -> none  [local(): pl.pallas_call(functools.partial(kernel, cfg), out_shape=jax.ShapeDtypeSt...]
    pallas_call x1, Pallas kernels: 27.2 us -> 26.5 us  [local(): pl.pallas_call(functools.partial(kernel, cfg), out_shape=jax.ShapeDtypeSt...]
where the time goes in v2:
time: 28.1 us; the launch traced here: 27.9 us
  Pallas kernels  26.5 us (94%)
  local copies, waits for them, and re-layouts  1.39 us (5%)
    pallas_call x1, Pallas kernels, local(): pl.pallas_call(functools.partial(kernel, cfg), out_shape=jax.ShapeDtypeSt...  26.5 us
    unnamed x1, local copies, waits for them, and re-layouts  1.39 us

profile of v2, /device:TPU:1, one launch (start us, length us, event | category | flops | bytes accessed | tf_op | source)
XLA Modules:
  0.0 27.9 jit_solution(15324738950230470145)
XLA Ops:
  0.0 26.5 %shard_map.118 = f32[1,3,4,642]{3,2,1,0:T(4,128)} custom-call(s32[1,2]{1,0:T(1,128)} %pair_target.1, s32[1,2]{1,0:T(1,128)} %pair_source.1, s32[1,1,4]{2,1,0:T(1,128)} %junction_cell.1, s32[1,1,4]{2,1,0:T(1,128)} %junction_target.1, s32[1,2,4]{2,1,0:T(2,128)} %bitcast.7, bf16[1,3,4,642]{3,2,1,0:T(4,128)(2,1)} %bitcast.5, bf16[1,3,4,642]{3,2,1,0:T(4,128)(2,1)} %bitcast.6, ...), custom_call_target="tpu_custom_call" | custom-call | tf_op jit(solution)/shard_map/pallas_call | solution.py:292
  26.5 1.4 %copy.14 = f32[1,4,3,642]{3,1,2,0:T(4,128)} copy(f32[1,4,3,642]{3,1,2,0:T(4,128)} %bitcast.4) | data formatting | bytes 61632

commit v3 on v2

--- a/solution.py
+++ b/solution.py
@@ -34,9 +34,10 @@
 
 def kernel(
     cfg,
-    pair_target, pair_source, junction_cell, junction_target, wall_near,
-    positions, density, upsample, quad, coarse, wall_points, wall_traction,
+    pair_target_far, pair_source_far, junction_cell_far, junction_target_far, wall_near_far,
+    positions, density, upsample, quad_far, coarse_far, wall_points, wall_traction,
     out,
+    pair_target, pair_source, junction_cell, junction_target, wall_near, quad, coarse,
     own, low, high, jsend, jrecv, walls, ups, rows, lhs, fine, ysrc, gsrc, yd, yg, ga, gb, xt, xs, wide, acc,
     local_sem, halo_send, halo_recv, junction_send, junction_recv, wall_send, wall_recv,
 ):
@@ -45,6 +46,12 @@
     rows_t = up(points, 16)
     seg, slab = lax.axis_index("seg"), lax.axis_index("slab")
 
+    barrier = pltpu.get_barrier_semaphore()
+    for o in range(1, segs):
+        pl.semaphore_signal(barrier, inc=1, device_id={"seg": lax.rem(seg + o, segs)}, device_id_type=MESH)
+    for o in range(1, slabs):
+        pl.semaphore_signal(barrier, inc=1, device_id={"slab": lax.rem(slab + o, slabs)}, device_id_type=MESH)
+
     copies = [
         pltpu.make_async_copy(positions.at[0], own.at[0], local_sem.at[0]),
         pltpu.make_async_copy(density.at[0], own.at[1], local_sem.at[1]),
@@ -52,17 +59,16 @@
         pltpu.make_async_copy(wall_traction.at[0], walls.at[pl.ds(slab * per_slab, per_slab), 1], local_sem.at[3]),
     ]
     big = pltpu.make_async_copy(upsample, ups, local_sem.at[4])
-    for copy in copies:
+    tables = [
+        pltpu.make_async_copy(source, target, local_sem.at[5 + i]) for i, (source, target) in enumerate([
+            (pair_target_far, pair_target), (pair_source_far, pair_source), (junction_cell_far, junction_cell),
+            (junction_target_far, junction_target), (wall_near_far, wall_near), (quad_far, quad), (coarse_far, coarse)])
+    ]
+    for copy in copies + tables:
         copy.start()
     big.start()
 
-    barrier = pltpu.get_barrier_semaphore()
-    for o in range(1, segs):
-        pl.semaphore_signal(barrier, inc=1, device_id={"seg": lax.rem(seg + o, segs)}, device_id_type=MESH)
-    for o in range(1, slabs):
-        pl.semaphore_signal(barrier, inc=1, device_id={"slab": lax.rem(slab + o, slabs)}, device_id_type=MESH)
-
-    for copy in copies:
+    for copy in copies + tables:
         copy.wait()
     cell_at = lax.broadcasted_iota(jnp.int32, (count, points), 0)
 
@@ -87,52 +93,11 @@
     def _():
         high[...] = jnp.zeros_like(high)
 
-    pl.semaphore_wait(barrier, segs - 1 + slabs - 1)
-
-    def halo_up():
-        return pltpu.make_async_remote_copy(
-            own, low, halo_send.at[0], halo_recv.at[0],
-            device_id={"slab": lax.rem(slab + 1, slabs)}, device_id_type=MESH)
-
-    def halo_down():
-        return pltpu.make_async_remote_copy(
-            own, high, halo_send.at[1], halo_recv.at[1],
-            device_id={"slab": lax.rem(slab + slabs - 1, slabs)}, device_id_type=MESH)
-
-    def junction(o):
-        return pltpu.make_async_remote_copy(
-            jsend.at[lax.rem(seg + o, segs)], jrecv.at[seg], junction_send.at[o], junction_recv.at[o],
-            device_id={"seg": lax.rem(seg + o, segs)}, device_id_type=MESH)
-
-    def junction_in(o):
-        return pltpu.make_async_remote_copy(
-            jsend.at[seg], jrecv.at[lax.rem(seg + segs - o, segs)], junction_send.at[o], junction_recv.at[o],
-            device_id={"seg": lax.rem(seg + o, segs)}, device_id_type=MESH)
-
-    def wall(o, of):
-        slot = pl.ds(of * per_slab, per_slab)
-        return pltpu.make_async_remote_copy(
-            walls.at[slot], walls.at[slot], wall_send.at[o], wall_recv.at[o],
-            device_id={"slab": lax.rem(slab + o, slabs)}, device_id_type=MESH)
-
-    @pl.when(slab < slabs - 1)
-    def _():
-        halo_up().start()
-
-    @pl.when(slab > 0)
-    def _():
-        halo_down().start()
-
-    for o in range(1, segs):
-        junction(o).start()
-    for o in range(slabs - 1, 0, -1):
-        wall(o, slab).start()
-
     rows[...] = jnp.zeros_like(rows)
     coords = [own[0, i].astype(F32) for i in range(3)]
     norms = split(KAPPA * (coords[0] * coords[0] + coords[1] * coords[1] + coords[2] * coords[2]), 3)
     rows[9:12, 0:points] = jnp.ones((3, points), F32)
-    for c in range(count):
+    def target_rows(c):
         for i in range(3):
             line = coords[i][c:c + 1]
             xs[c, i:i + 1] = line
@@ -144,6 +109,52 @@
         for i in range(3):
             wide[c, i] = jnp.broadcast_to(turned[:, i:i + 1], (rows_t, LANES))
         acc[c] = jnp.zeros(acc.shape[1:], F32)
+
+    for c in range(count // 2):
+        target_rows(c)
+    pl.semaphore_wait(barrier, segs - 1 + slabs - 1)
+
+    def halo_up():
+        return pltpu.make_async_remote_copy(
+            own, low, halo_send.at[0], halo_recv.at[0],
+            device_id={"slab": lax.rem(slab + 1, slabs)}, device_id_type=MESH)
+
+    def halo_down():
+        return pltpu.make_async_remote_copy(
+            own, high, halo_send.at[1], halo_recv.at[1],
+            device_id={"slab": lax.rem(slab + slabs - 1, slabs)}, device_id_type=MESH)
+
+    def junction(o):
+        return pltpu.make_async_remote_copy(
+            jsend.at[lax.rem(seg + o, segs)], jrecv.at[seg], junction_send.at[o], junction_recv.at[o],
+            device_id={"seg": lax.rem(seg + o, segs)}, device_id_type=MESH)
+
+    def junction_in(o):
+        return pltpu.make_async_remote_copy(
+            jsend.at[seg], jrecv.at[lax.rem(seg + segs - o, segs)], junction_send.at[o], junction_recv.at[o],
+            device_id={"seg": lax.rem(seg + o, segs)}, device_id_type=MESH)
+
+    def wall(o, of):
+        slot = pl.ds(of * per_slab, per_slab)
+        return pltpu.make_async_remote_copy(
+            walls.at[slot], walls.at[slot], wall_send.at[o], wall_recv.at[o],
+            device_id={"slab": lax.rem(slab + o, slabs)}, device_id_type=MESH)
+
+    @pl.when(slab < slabs - 1)
+    def _():
+        halo_up().start()
+
+    @pl.when(slab > 0)
+    def _():
+        halo_down().start()
+
+    for o in range(1, segs):
+        junction(o).start()
+    for o in range(slabs - 1, 0, -1):
+        wall(o, slab).start()
+
+    for c in range(count // 2, count):
+        target_rows(c)
 
     def prepare(start, size):
         at = pl.ds(start, size)
@@ -175,7 +186,8 @@
         targets = xt[target]
         ats = [pl.ds(pl.multiple_of(start + i * LANES, LANES), LANES) for i in range(size)]
         total = None
-        for i in range(0, size - 1, 2):
+        single = {7: 3, 6: 2}.get(size, size % 2)
+        for i in range(0, size - single, 2):
             pair = jnp.dot(
                 targets, jnp.concatenate([yd[:, ats[i]], yd[:, ats[i + 1]]], axis=1), preferred_element_type=F32)
             for at, distance in ((ats[i], pair[:, :LANES]), (ats[i + 1], pair[:, LANES:])):
@@ -184,8 +196,7 @@
                 along = along + wide[target, 2] * gsrc[2:3, at]
                 term = finish(distance, along, at)
                 total = term if total is None else total + term
-        if size % 2:
-            at = ats[-1]
+        for at in ats[size - single:]:
             both = jnp.dot(
                 targets, jnp.concatenate([yd[:, at], yg[:, at]], axis=1), preferred_element_type=F32)
             term = finish(both[:, :LANES], both[:, LANES:], at)
@@ -193,7 +204,7 @@
         return total
 
     def block(target, start, chunks):
-        size = 3 if chunks % 3 == 0 else (2 if chunks % 2 == 0 else 1)
+        size = max(n for n in range(1, 8) if chunks % n == 0)
 
         def step(i, total):
             return total + group(target, start + i * size * LANES, size)
@@ -285,16 +296,22 @@
     cfg = (count, points, fine_points, pairs, near, patch, segs, slabs, per_slab)
     pt, qp = up(points, LANES), up(fine_points, LANES)
     lanes = pairs * qp + (segs - 1) * pt + count * near * up(patch, LANES)
-    smem = pl.BlockSpec(memory_space=pltpu.SMEM)
     vmem = pl.BlockSpec(memory_space=pltpu.VMEM)
     far = pl.BlockSpec(memory_space=pl.ANY)
     dma = pltpu.SemaphoreType.DMA
     result = pl.pallas_call(
         functools.partial(kernel, cfg),
         out_shape=jax.ShapeDtypeStruct(turned, F32),
-        in_specs=[smem] * 5 + [far, far, far, vmem, vmem, far, far],
+        in_specs=[far] * 12,
         out_specs=vmem,
         scratch_shapes=[
+            pltpu.SMEM(pair_target.shape, jnp.int32),
+            pltpu.SMEM(pair_source.shape, jnp.int32),
+            pltpu.SMEM(junction_cell.shape, jnp.int32),
+            pltpu.SMEM(junction_target.shape, jnp.int32),
+            pltpu.SMEM((1, near, count), jnp.int32),
+            pltpu.VMEM(quad_weights.shape, F32),
+            pltpu.VMEM(coarse_weights.shape, F32),
             pltpu.VMEM((2,) + turned[1:], BF16),
             pltpu.VMEM((2,) + turned[1:], BF16),
             pltpu.VMEM((2,) + turned[1:], BF16),
@@ -315,7 +332,7 @@
             pltpu.VMEM((count, 3, points), F32),
             pltpu.VMEM((count, 3, up(points, 16), LANES), F32),
             pltpu.VMEM((count, TERMS, up(points, 16)), F32),
-            dma((5,)), dma((2,)), dma((2,)), dma((segs,)), dma((segs,)), dma((slabs,)), dma((slabs,)),
+            dma((12,)), dma((2,)), dma((2,)), dma((segs,)), dma((segs,)), dma((slabs,)), dma((slabs,)),
         ],
         compiler_params=pltpu.CompilerParams(collective_id=0, has_side_effects=True),
     )(pair_target, pair_source, junction_cell, junction_target, wall_near.transpose(0, 2, 1),

time: 28.1 us -> 24.8 us (0.88)
  Pallas kernels: 26.5 us -> 23.2 us
    pallas_call x1, Pallas kernels: 26.5 us -> 23.2 us  [local(): pl.pallas_call(functools.partial(kernel, cfg), out_shape=jax.ShapeDtypeSt...]
where the time goes in v3:
time: 24.8 us; the launch traced here: 24.6 us
  Pallas kernels  23.2 us (94%)
  local copies, waits for them, and re-layouts  1.39 us (6%)
    pallas_call x1, Pallas kernels, local(): pl.pallas_call(functools.partial(kernel, cfg), out_shape=jax.ShapeDtypeSt...  23.2 us
    unnamed x1, local copies, waits for them, and re-layouts  1.39 us

profile of v3, /device:TPU:1, one launch (start us, length us, event | category | flops | bytes accessed | tf_op | source)
XLA Modules:
  0.0 24.6 jit_solution(13460192174950495503)
XLA Ops:
  0.0 23.2 %shard_map.118 = f32[1,3,4,642]{3,2,1,0:T(4,128)} custom-call(s32[1,2]{1,0:T(1,128)} %pair_target_far.1, s32[1,2]{1,0:T(1,128)} %pair_source_far.1, s32[1,1,4]{2,1,0:T(1,128)} %junction_cell_far.1, s32[1,1,4]{2,1,0:T(1,128)} %junction_target_far.1, s32[1,2,4]{2,1,0:T(2,128)} %bitcast.7, bf16[1,3,4,642]{3,2,1,0:T(4,128)(2,1)} %bitcast.5, ...), custom_call_target="tpu_custom_call" | custom-call | tf_op jit(solution)/shard_map/pallas_call | solution.py:302
  23.2 1.4 %copy.14 = f32[1,4,3,642]{3,1,2,0:T(4,128)} copy(f32[1,4,3,642]{3,1,2,0:T(4,128)} %bitcast.4) | data formatting | bytes 61632

commit v4 on v3

--- a/solution.py
+++ b/solution.py
@@ -14,6 +14,7 @@
 WALL_GAIN = 3.0
 LANES = 128
 TERMS = 16
+MOST = 7
 KAPPA = 1.0 / EPSILON2
 F32 = jnp.float32
 BF16 = jnp.bfloat16
@@ -237,9 +238,16 @@
         ysrc[0:3, pl.ds(k * qp, fine_points)] = fine[6 * k:6 * k + 3]
         gsrc[0:3, pl.ds(k * qp, fine_points)] = fine[6 * k + 3:6 * k + 6] * quad[...][None]
     prepare(0, pairs * qp)
+    size = max(n for n in range(1, MOST + 1) if (qp // LANES) % n == 0)
+
+    def together(i, totals):
+        return tuple(
+            total + group(pair_target[0, k], k * qp + i * size * LANES, size) for k, total in enumerate(totals))
+
+    zero = jnp.zeros((TERMS, rows_t), F32)
+    totals = lax.fori_loop(0, qp // LANES // size, together, (zero,) * pairs)
     for k in range(pairs):
-        target = pair_target[0, k]
-        add(target, block(target, k * qp, qp // LANES))
+        add(pair_target[0, k], totals[k])
 
     base = pairs * qp
     for o in range(1, segs):

time: 24.8 us -> 23.5 us (0.948)
  Pallas kernels: 23.2 us -> 21.8 us
    pallas_call x1, Pallas kernels: 23.2 us -> 21.8 us  [local(): pl.pallas_call(functools.partial(kernel, cfg), out_shape=jax.ShapeDtypeSt...]
where the time goes in v4:
time: 23.5 us; the launch traced here: 23.2 us
  Pallas kernels  21.8 us (93%)
  local copies, waits for them, and re-layouts  1.39 us (6%)
    pallas_call x1, Pallas kernels, local(): pl.pallas_call(functools.partial(kernel, cfg), out_shape=jax.ShapeDtypeSt...  21.8 us
    unnamed x1, local copies, waits for them, and re-layouts  1.39 us

profile of v4, /device:TPU:1, one launch (start us, length us, event | category | flops | bytes accessed | tf_op | source)
XLA Modules:
  0.0 23.2 jit_solution(6047436281118966045)
XLA Ops:
  0.0 21.8 %shard_map.118 = f32[1,3,4,642]{3,2,1,0:T(4,128)} custom-call(s32[1,2]{1,0:T(1,128)} %pair_target_far.1, s32[1,2]{1,0:T(1,128)} %pair_source_far.1, s32[1,1,4]{2,1,0:T(1,128)} %junction_cell_far.1, s32[1,1,4]{2,1,0:T(1,128)} %junction_target_far.1, s32[1,2,4]{2,1,0:T(2,128)} %bitcast.7, bf16[1,3,4,642]{3,2,1,0:T(4,128)(2,1)} %bitcast.5, ...), custom_call_target="tpu_custom_call" | custom-call | tf_op jit(solution)/shard_map/pallas_call | solution.py:310
  21.9 1.4 %copy.14 = f32[1,4,3,642]{3,1,2,0:T(4,128)} copy(f32[1,4,3,642]{3,1,2,0:T(4,128)} %bitcast.4) | data formatting | bytes 61632
